TPU v7x, 512 devices: a whole 4x8x8 slice. The times are simulated.
512 devices in a mesh: dp: 16 (over y, core), expert: 32 (over x, z).
Axes of the slice: x: 4, y: 8, z: 8, core: 2. Of those that a mesh axis runs over, the one named last changes fastest.
Arguments:
- attention: bfloat16 [65536, 1536], P(('dp', 'expert')), may hold values from -6 to 6
- residual: bfloat16 [65536, 1536], P(('dp', 'expert')), may hold values from -6 to 6
- out_weight: bfloat16 [1536, 1536], P(('dp', 'expert')), may hold values from -0.15625 to 0.15625
- gate_weight: bfloat16 [32, 1536, 512], P('expert', 'dp'), may hold values from -0.15625 to 0.15625
- up_weight: bfloat16 [32, 1536, 512], P('expert', 'dp'), may hold values from -0.15625 to 0.15625
- down_weight: bfloat16 [32, 512, 1536], P('expert'), may hold values from -0.25 to 0.25
- routes: int32 [65536, 8], P(('dp', 'expert')), may hold values from 0 to 31, all different within a row; in each aligned block of 128 rows (0 to 127, 128 to 255, ...) at most 40 rows name the same one
- router_scores: float32 [65536, 8], P(('dp', 'expert')), may hold values from 0.05 to 1
- norm_gain: float32 [1536], replicated, may hold values from 0.5 to 1.5
Outputs:
- normed: bfloat16 [65536, 1536], P(('dp', 'expert'))
Inputs may be any that keep to these rules, and one draw needn't show every extreme that they name: `routes`: in each aligned block of 128 rows (the rows of one device) no expert is named by more than 40 rows, a bound that some block reaches; a row names 8 different experts.
All inputs are finite; a program needn't handle non-finite values.
Results may differ from a plain program's by a relative error of at most 0.0053.
Values may be sent and summed in bfloat16 or wider, within the bound.
A program may use at most 64 MiB of HBM per device.

v0:
```python
import jax
import jax.numpy as jnp
from jax import lax
from jax.sharding import PartitionSpec as P


def body(
    attention,
    residual,
    out_weight,
    gate_weight,
    up_weight,
    down_weight,
    routes,
    router_scores,
    norm_gain,
):
    token_count, feature_count = attention.shape
    chosen = routes.shape[1]
    full_weight = lax.all_gather(out_weight, ("dp", "expert"), axis=0, tiled=True)
    projected = jnp.dot(attention, full_weight, preferred_element_type=jnp.float32)
    stream = (residual.astype(jnp.float32) + projected).astype(jnp.bfloat16)
    gate_full, up_full = (
        lax.all_gather(gate_weight, "dp", axis=1, tiled=True),
        lax.all_gather(up_weight, "dp", axis=1, tiled=True),
    )
    gate_mat = gate_full[0]
    up_mat = up_full[0]
    down_mat = down_weight[0]
    peers = lax.axis_size("expert")
    capacity = min(token_count, token_count * chosen * 5 // (4 * peers))
    pairs = routes.reshape(-1)
    onehot = (pairs[:, None] == jnp.arange(peers, dtype=jnp.int32)[None, :]).astype(jnp.int32)
    earlier = jnp.cumsum(onehot, axis=0) - onehot
    position = jnp.sum(earlier * onehot, axis=1)
    target = pairs * capacity + position
    token_index = jnp.arange(token_count * chosen, dtype=jnp.int32) // chosen
    table = jnp.full((peers * capacity,), token_count, jnp.int32).at[target].set(token_index)
    padded = jnp.concatenate([stream, jnp.zeros((1, feature_count), jnp.bfloat16)], axis=0)
    outgoing = padded[table].reshape(peers, capacity, feature_count)
    received = lax.all_to_all(outgoing, "expert", split_axis=0, concat_axis=0, tiled=True)
    rows_in = received.reshape(-1, feature_count)
    gate_act = jnp.dot(rows_in, gate_mat, preferred_element_type=jnp.float32)
    up_act = jnp.dot(rows_in, up_mat, preferred_element_type=jnp.float32)
    expert_hidden = (jax.nn.silu(gate_act) * up_act).astype(jnp.bfloat16)
    expert_out = jnp.dot(expert_hidden, down_mat, preferred_element_type=jnp.float32).astype(
        jnp.bfloat16
    )
    answered = lax.all_to_all(
        expert_out.reshape(received.shape), "expert", split_axis=0, concat_axis=0, tiled=True
    )
    picked = answered.reshape(-1, feature_count)[target].reshape(token_count, chosen, feature_count)
    combine = router_scores / jnp.sum(router_scores, axis=1, keepdims=True)
    mixture = jnp.zeros((token_count, feature_count), jnp.float32)
    for choice_index in range(chosen):
        mixture = mixture + combine[:, choice_index : choice_index + 1] * picked[
            :, choice_index
        ].astype(jnp.float32)
    total = stream.astype(jnp.float32) + mixture
    scale = lax.rsqrt(jnp.mean(total * total, axis=1, keepdims=True) + 1e-06)
    return (total * scale * norm_gain[None, :]).astype(jnp.bfloat16)


def solution(mesh):
    in_specs = (
        P(("dp", "expert"), None),
        P(("dp", "expert"), None),
        P(("dp", "expert"), None),
        P("expert", "dp", None),
        P("expert", "dp", None),
        P("expert", None, None),
        P(("dp", "expert"), None),
        P(("dp", "expert"), None),
        P(),
    )
    out_specs = P(("dp", "expert"), None)
    return jax.shard_map(body, mesh=mesh, in_specs=in_specs, out_specs=out_specs, check_vma=False)
```

profile of v0, /device:TPU:1, one launch (start us, length us, event | category | flops | bytes accessed | tf_op | source)
XLA Modules:
  0.0 402.0 jit_solution(10342804823268837833)
XLA Ops:
  7.4 0.7 all-gather.9.cloned.1.call-update
  8.1 0.8 copy.24
  8.9 0.1 eq.29
  9.0 0.1 eq.25
  9.1 9.0 %reduce-window.6 = s32[32,8,128]{2,1,0:T(8,128)S(1)} reduce-window(s32[32,8,128]{2,1,0:T(8,128)S(1)} %fusion.19, s32[]{:T(128)} %constant.35.clone.1), window={size=1x1x128 pad=0_0x0_0x127_0}, to_apply=%region_1.2 | reduce-window | flops 4161536 | bytes 262148 | tf_op jit(solution)/shard_map/reduce-window
  18.1 0.1 slice.76
  18.2 0.1 copy.26
  18.4 0.1 copy.27
  18.4 0.7 broadcast_multiply_fusion
  19.1 0.1 copy.23
  19.2 0.1 mul.129
  19.4 0.1 broadcast_add_fusion
  19.5 4.3 %scatter_custom_fusion = s32[1280]{0:T(1024)S(1)} fusion(s32[1024]{0:T(1024)S(1)} %bitcast.111, s32[1024]{0:T(1024)S(1)} %add_select_fusion, s32[]{:T(128)} %constant.33.clone.1), kind=kCustom, calls=%fused_computation.55 | custom fusion | bytes 5124 | tf_op jit(solution)/shard_map/scatter | solution.py:38
  23.9 116.2 %all-gather.9.cloned.1.call-done = bf16[512,3,1536]{2,1,0:T(4,128)(2,1)} async-done(((bf16[1,3,1536]{2,1,0:T(4,128)(2,1)}), bf16[512,3,1536]{2,1,0:T(4,128)(2,1)}) %all-gather.9.cloned.1.call-update) | async-done | bytes 4718608 | tf_op jit(solution)/shard_map/all_gather | solution.py:20
  140.1 12.3 %reshape.127 = bf16[1536,1536]{1,0:T(8,128)(2,1)} reshape(bf16[512,3,1536]{2,1,0:T(4,128)(2,1)} %all-gather.9.cloned.1.call-done) | data formatting | bytes 9437184
  152.5 3.1 fusion.1
  155.6 5.5 %gather_fusion = bf16[1280,1536]{1,0:T(8,128)(2,1)} fusion(bf16[129,1536]{1,0:T(8,128)(2,1)S(1)} %concatenate.3, s32[2048]{0:T(1024)S(1)} %pad_clamp_fusion), kind=kCustom, calls=%fused_computation | custom fusion | bytes 7869440 | tf_op jit(solution)/shard_map/gather | solution.py:40
  161.1 7.8 %all-to-all-start = ((bf16[32,40,1536]{2,1,0:T(8,128)(2,1)}), bf16[32,40,1536]{2,1,0:T(8,128)(2,1)}, u32[]{:S(2)}, u32[]{:S(2)}) async-start(bf16[32,40,1536]{2,1,0:T(8,128)(2,1)} %bitcast.106), calls=%async_computation | async-start | bytes 7864320 | tf_op jit(solution)/shard_map/all_to_all | solution.py:41
  168.9 0.0 all-gather.5.cloned.1.call-start
  168.9 0.5 all-gather.5.cloned.1.call-update
  169.4 0.0 all-gather.7.cloned.1.call-start
  169.5 0.5 all-gather.7.cloned.1.call-update
  170.0 41.7 %all-gather.5.cloned.1.call-done = bf16[1,1536,512]{2,1,0:T(8,128)(2,1)} async-done(((bf16[1,96,512]{2,1,0:T(8,128)(2,1)}), bf16[1,1536,512]{2,1,0:T(8,128)(2,1)}) %all-gather.5.cloned.1.call-update) | async-done | bytes 1572880 | tf_op jit(solution)/shard_map/all_gather | solution.py:24
  211.7 45.4 %all-to-all-done = bf16[32,40,1536]{2,1,0:T(8,128)(2,1)} async-done(((bf16[32,40,1536]{2,1,0:T(8,128)(2,1)}), bf16[32,40,1536]{2,1,0:T(8,128)(2,1)}, u32[]{:S(2)}, u32[]{:S(2)}) %all-to-all-start) | async-done | bytes 3932192 | tf_op jit(solution)/shard_map/all_to_all | solution.py:41
  257.2 6.3 %fusion.4 = f32[1280,512]{1,0:T(8,128)} fusion(bf16[1280,1536]{1,0:T(8,128)(2,1)} %bitcast.7, bf16[1,1536,512]{2,1,0:T(8,128)(2,1)} %all-gather.5.cloned.1.call-done), kind=kOutput, calls=%fused_computation.10 | convolution fusion | flops 2013265920 | bytes 8126464 | tf_op jit(solution)/shard_map/dot_general | solution.py:43
  263.5 9.6 %convolution_convert_fusion = bf16[1280,1536]{1,0:T(8,128)(2,1)} fusion(bf16[1,512,1536]{2,1,0:T(8,128)(2,1)S(1)} %copy-done, bf16[1280,1536]{1,0:T(8,128)(2,1)} %bitcast.7, f32[1280,512]{1,0:T(8,128)} %fusion.4, bf16[1,1536,512]{2,1,0:T(8,128)(2,1)} %all-gather.7.cloned.1.call-done), kind=kOutput, calls=%fused_computation.3 | convolution fusion | flops 4032430080 | bytes 13631488 | tf_op jit(solution)/shard_map/dot_general | solution.py:46
  273.2 8.6 %all-to-all-start.1 = ((bf16[32,40,1536]{2,1,0:T(8,128)(2,1)}), bf16[32,40,1536]{2,1,0:T(8,128)(2,1)}, u32[]{:S(2)}, u32[]{:S(2)}) async-start(bf16[32,40,1536]{2,1,0:T(8,128)(2,1)} %bitcast.107), calls=%async_computation.1 | async-start | bytes 7864320 | tf_op jit(solution)/shard_map/all_to_all | solution.py:49
  281.8 86.7 %all-to-all-done.1 = bf16[32,40,1536]{2,1,0:T(8,128)(2,1)} async-done(((bf16[32,40,1536]{2,1,0:T(8,128)(2,1)}), bf16[32,40,1536]{2,1,0:T(8,128)(2,1)}, u32[]{:S(2)}, u32[]{:S(2)}) %all-to-all-start.1) | async-done | bytes 3932192 | tf_op jit(solution)/shard_map/all_to_all | solution.py:49
  368.6 9.9 %gather_fusion.1 = bf16[1024,1536]{1,0:T(8,128)(2,1)} fusion(bf16[1280,1536]{1,0:T(8,128)(2,1)} %bitcast.12, s32[1024]{0:T(1024)S(1)} %broadcast_clamp_fusion), kind=kCustom, calls=%fused_computation.1 | custom fusion | bytes 6295552 | tf_op jit(solution)/shard_map/gather | solution.py:52
  378.5 14.2 %fusion.27 = (bf16[128,1,1536]{2,1,0:T(2,128)(2,1)S(1)}, bf16[128,1,1536]{2,1,0:T(2,128)(2,1)S(1)}, bf16[128,1,1536]{2,1,0:T(2,128)(2,1)S(1)}, bf16[128,1,1536]{...) fusion(bf16[128,8,1536]{2,1,0:T(8,128)(2,1)} %bitcast.105), kind=kLoop, calls=%fused_computation.71 | loop fusion | bytes 6291456 | tf_op jit(solution)/shard_map/slice | solution.py:56
  392.7 0.9 multiply_reduce_fusion
  393.6 0.9 multiply_convert_fusion
  (26 shorter events, 0.2 us)
Async XLA Ops:
  7.4 256.1 %copy-start = (bf16[1,512,1536]{2,1,0:T(8,128)(2,1)S(1)}, bf16[1,512,1536]{2,1,0:T(8,128)(2,1)}, u32[]{:S(2)}) copy-start(bf16[1,512,1536]{2,1,0:T(8,128)(2,1)} %param.14) | copy-start | bytes 4718596
  7.4 132.7 %all-gather.9.cloned.1.call-start = ((), (), s32[]{:S(2)}) async-start(), calls=%async_computation.4 | async-start | bytes 6303744 | tf_op jit(solution)/shard_map/all_gather | solution.py:20
  23.9 128.6 %copy-start.1 = (bf16[128,1536]{1,0:T(8,128)(2,1)S(1)}, bf16[128,1536]{1,0:T(8,128)(2,1)}, u32[]{:S(2)}) copy-start(bf16[128,1536]{1,0:T(8,128)(2,1)} %param.9) | copy-start | bytes 1179652
  23.9 128.6 %copy-start.2 = (bf16[128,1536]{1,0:T(8,128)(2,1)S(1)}, bf16[128,1536]{1,0:T(8,128)(2,1)}, u32[]{:S(2)}) copy-start(bf16[128,1536]{1,0:T(8,128)(2,1)} %param.10) | copy-start | bytes 1179652
  161.1 96.1 %all-to-all-start = ((bf16[32,40,1536]{2,1,0:T(8,128)(2,1)}), bf16[32,40,1536]{2,1,0:T(8,128)(2,1)}, u32[]{:S(2)}, u32[]{:S(2)}) async-start(bf16[32,40,1536]{2,1,0:T(8,128)(2,1)} %bitcast.106), calls=%async_computation | async-start | bytes 7864320 | tf_op jit(solution)/shard_map/all_to_all | solution.py:41
  168.9 42.9 %all-gather.5.cloned.1.call-start = ((), (), s32[]{:S(2)}) async-start(), calls=%async_computation.2 | async-start | bytes 1671168 | tf_op jit(solution)/shard_map/all_gather | solution.py:24
  169.4 94.1 %all-gather.7.cloned.1.call-start = ((), (), s32[]{:S(2)}) async-start(), calls=%async_computation.3 | async-start | bytes 1671168 | tf_op jit(solution)/shard_map/all_gather | solution.py:25
  273.2 8.6 %copy-start.3 = (f32[128,8]{0,1:T(8,128)S(1)}, f32[128,8]{0,1:T(8,128)}, u32[]{:S(2)}) copy-start(f32[128,8]{0,1:T(8,128)} %param.16) | copy-start | bytes 12292
  273.2 95.4 %all-to-all-start.1 = ((bf16[32,40,1536]{2,1,0:T(8,128)(2,1)}), bf16[32,40,1536]{2,1,0:T(8,128)(2,1)}, u32[]{:S(2)}, u32[]{:S(2)}) async-start(bf16[32,40,1536]{2,1,0:T(8,128)(2,1)} %bitcast.107), calls=%async_computation.1 | async-start | bytes 7864320 | tf_op jit(solution)/shard_map/all_to_all | solution.py:49
  392.7 0.9 copy-start.4
Sparse Core Ops, SparseCore 0:
  12.4 127.6 all-gather.8
Sparse Core Ops, SparseCore 1:
  171.5 40.2 all-gather.4
  213.7 40.5 all-gather.6
where the time goes:
time: 405 us; the launch traced here: 402 us
  waiting for transfers between devices  292 us (72%)
  local copies, waits for them, and re-layouts  47.8 us (12%)
  matrix products  19.1 us (5%)
  starting transfers between devices  16.5 us (4%)
  between operations  15 us (4%)
  other arithmetic  11.7 us (3%)
    all_gather x1, waiting for transfers between devices, body(): lax.all_gather(out_weight, ('dp', 'expert'), axis=0, tiled=True)  116 us
    all_to_all x1, waiting for transfers between devices, body(): lax.all_to_all(expert_out.reshape(received.shape), 'expert', split_axis=0...  86.7 us
    all_to_all x1, waiting for transfers between devices, body(): lax.all_to_all(outgoing, 'expert', split_axis=0, concat_axis=0, tiled=True)  45.4 us
    all_gather x1, waiting for transfers between devices, body(): lax.all_gather(gate_weight, 'dp', axis=1, tiled=True)  41.7 us
    slice x1, local copies, waits for them, and re-layouts, body(): picked[:, choice_index].astype(jnp.float32)  14.2 us
    unnamed x12, local copies, waits for them, and re-layouts  13.1 us
    gather x1, local copies, waits for them, and re-layouts, body(): answered.reshape(-1, feature_count)[target]  9.9 us
    dot_general x1, matrix products, body(): jnp.dot(expert_hidden, down_mat, preferred_element_type=jnp.float32)  9.65 us
  transfers between devices with their start and end apart: 5, of which 4 were waited for; matrix products, arithmetic and copies ran while one was open for 5% of the time, Pallas kernels for 0%

commit v1 on v0

v1 whole, which is shorter than its diff:
```python
import jax
import jax.numpy as jnp
import numpy as np
from jax import lax
from jax.experimental import pallas as pl
from jax.experimental.pallas import tpu as pltpu
from jax.sharding import PartitionSpec as P

NX, NY, NZ = 4, 8, 8
CAP = 40
PAIR = 2 * CAP
SLOT = {0: 0, 4: 1, 1: 2, -1: 3, 2: 4, -2: 5, 3: 6, -3: 7}


def rel_slot(r):
    r = r % NZ
    return SLOT[r if r <= 4 else r - NZ]


class Net:
    def __init__(self, send_sems, recv_sems):
        self.ss, self.rs, self.count, self.sent = send_sems, recv_sems, 0, []

    def send(self, src, dst, device):
        i = self.count
        self.count += 1
        copy = pltpu.make_async_remote_copy(
            src_ref=src, dst_ref=dst, send_sem=self.ss.at[i], recv_sem=self.rs.at[i],
            device_id=device, device_id_type=pl.DeviceIdType.MESH,
        )
        copy.start()
        self.sent.append(copy)
        return i

    def arrive(self, i, region, device):
        pltpu.make_async_remote_copy(
            src_ref=region, dst_ref=region, send_sem=self.ss.at[i], recv_sem=self.rs.at[i],
            device_id=device, device_id_type=pl.DeviceIdType.MESH,
        ).wait_recv()

    def drain(self):
        for copy in self.sent:
            copy.wait_send()


N_COPIES = 140


def kernel(
    att, res, ow, gate, up, down, routes_t, scores_t, gain, kperm,
    out,
    s1, s1f, OW, G, U, DN, tok, meta, tab, sel, wrow, X, Y, SB, RB, part, aperm,
    send_sems, recv_sems, loc_sems,
):
    f32, bf16 = jnp.float32, jnp.bfloat16
    T, F = att.shape
    H = gate.shape[1]
    rows = gate.shape[0]
    dp, ex = lax.axis_index("dp"), lax.axis_index("expert")
    y, c = lax.div(dp, 2), lax.rem(dp, 2)
    x, z = lax.div(ex, NZ), lax.rem(ex, NZ)

    def md(a, n):
        return lax.rem(a + 2 * n, n)

    def dev(dx=0, dy=0, dz=0, other=False):
        cc = 1 - c if other else c
        return (md(y + dy, NY) * 2 + cc, md(x + dx, NX) * NZ + md(z + dz, NZ))

    partner = dev(other=True)
    barrier = pltpu.get_barrier_semaphore()
    peers = (
        [dev(dx=d) for d in range(1, NX)] + [dev(dy=d) for d in range(1, NY)]
        + [dev(dz=d) for d in range(1, NZ)] + [partner]
    )
    for p in peers:
        pl.semaphore_signal(barrier, inc=1, device_id=p, device_id_type=pl.DeviceIdType.MESH)
    pl.semaphore_wait(barrier, len(peers))

    net = Net(send_sems, recv_sems)

    def local(k, src, dst):
        copy = pltpu.make_async_copy(src, dst, loc_sems.at[k])
        copy.start()
        return copy

    own_ow = local(0, ow, s1.at[y, x])
    s1x = [(net.send(ow, s1.at[y, x], dev(dx=d)), d) for d in range(1, NX)]

    def wslice(W, e, yb, cc):
        return W.at[e, pl.ds(pl.multiple_of((yb * 2 + cc) * rows, 8), rows)]

    half = H // 2
    my_half = pl.ds(pl.multiple_of(c * half, 8), half)
    own_g = local(1, gate, wslice(G, x, y, c))
    own_u = local(2, up, wslice(U, x, y, c))
    own_d = local(3, down, DN.at[x])
    gux = []
    for d in (1, 3, 2):
        for src, W in ((gate, G), (up, U)):
            gux.append((net.send(src, wslice(W, x, y, c), dev(dx=d)), W, d))

    r8 = lax.broadcasted_iota(jnp.int32, (NZ * 8, T), 0)
    expert = (r8 % 4) * NZ + r8 // 8
    scores = scores_t[...]
    combine = scores / jnp.sum(scores, axis=0, keepdims=True)
    member = jnp.zeros((NZ * 8, T), f32)
    weight = jnp.zeros((NZ * 8, T), f32)
    for k in range(routes_t.shape[0]):
        hit = routes_t[k : k + 1, :] == expert
        member = member + jnp.where(hit, 1.0, 0.0)
        weight = weight + jnp.where(hit, combine[k : k + 1, :], 0.0)
    before = lax.broadcasted_iota(jnp.int32, (T, T), 0) < lax.broadcasted_iota(jnp.int32, (T, T), 1)
    place = jnp.dot(member.astype(bf16), jnp.where(before, 1.0, 0.0).astype(bf16), preferred_element_type=f32)
    table = jnp.where(r8 % 8 < 4, jnp.where(member > 0.5, place, -1000.0), weight)
    tab[...] = table.reshape(NZ, 8, T)
    meta[0] = tab[z]
    metas = []
    for d in range(1, NZ):
        metas.append((net.send(tab.at[md(z + d, NZ)], meta.at[rel_slot(-d)], dev(dz=d)), d))

    own_ow.wait()
    for i, d in s1x:
        net.arrive(i, s1.at[y, md(x - d, NX)], dev(dx=-d))
    s1y = [(net.send(s1.at[y], s1.at[y], dev(dy=d)), d) for d in range(1, NY)]

    dnx = []
    for d in (1, 3, 2):
        dnx.append((net.send(down.at[my_half], DN.at[x, my_half], dev(dx=d)), d))

    own_g.wait()
    own_u.wait()
    for i, W, d in gux:
        net.arrive(i, wslice(W, md(x - d, NX), y, c), dev(dx=-d))

    def wblock(W, yb, cc):
        return W.at[:, pl.ds(pl.multiple_of((yb * 2 + cc) * rows, 8), rows)]

    mats = (G, U)
    to_partner = []

    def share(k, yb):
        for W in mats:
            region = wblock(W, yb, c)
            to_partner.append((net.send(region, region, partner), W, yb))

    def wring_send(s):
        fwd, bwd = md(y - (s - 1), NY), md(y + (s - 1), NY)
        ids = []
        for m, W in enumerate(mats):
            if s < 4 or m == 0:
                ids.append((net.send(wblock(W, fwd, c), wblock(W, fwd, c), dev(dy=1)), W, md(y - s, NY), -1))
            if s < 4 or m == 1:
                ids.append((net.send(wblock(W, bwd, c), wblock(W, bwd, c), dev(dy=-1)), W, md(y + s, NY), 1))
        return ids

    def wring_arrive(ids):
        for i, W, yb, side in ids:
            net.arrive(i, wblock(W, yb, c), dev(dy=side))

    w_ids = wring_send(1)
    share(0, y)

    nt = F // 256

    def permute(j, carry):
        cols = pl.ds(pl.multiple_of(j * 256, 256), 256)
        onehot = lax.broadcasted_iota(jnp.int32, (F, 256), 0) == kperm[:, cols]
        aperm[:, cols] = jnp.dot(
            att[...], jnp.where(onehot, 1.0, 0.0).astype(bf16), preferred_element_type=f32
        ).astype(bf16)
        return carry

    lax.fori_loop(0, nt, permute, 0)

    for i, d in s1y:
        net.arrive(i, s1.at[md(y - d, NY)], dev(dy=-d))
    for yb in range(NY):
        for xb in range(NX):
            at = (yb * NX + xb) * 3
            s1f[at : at + 3, :] = s1[yb, xb].astype(f32)

    own_rows = NY * NX * 3

    def oblock(zb, cc, lo=0, n=own_rows):
        return OW.at[pl.ds(pl.multiple_of((zb * 2 + cc) * own_rows + lo, 8), n)]

    OW[pl.ds(pl.multiple_of((z * 2 + c) * own_rows, 8), own_rows), :] = s1f[...].astype(bf16)

    o_partner = []

    def oshare(zb):
        o_partner.append((net.send(oblock(zb, c), oblock(zb, c), partner), zb))

    def oring_send(s):
        fwd, bwd = md(z - (s - 1), NZ), md(z + (s - 1), NZ)
        lo, n = ((0, own_rows), (0, own_rows)) if s < 4 else ((0, own_rows // 2), (own_rows // 2, own_rows // 2)), None
        (flo, fn), (blo, bn) = lo
        a = net.send(oblock(fwd, c, flo, fn), oblock(fwd, c, flo, fn), dev(dz=1))
        b = net.send(oblock(bwd, c, blo, bn), oblock(bwd, c, blo, bn), dev(dz=-1))
        return [
            (a, oblock(md(z - s, NZ), c, flo, fn), -1),
            (b, oblock(md(z + s, NZ), c, blo, bn), 1),
        ]

    def ring_arrive(ids):
        for i, region, side in ids:
            net.arrive(i, region, dev(dz=side))

    o_ids = oring_send(1)
    oshare(z)
    ring_arrive(o_ids)
    o_ids = oring_send(2)
    oshare(md(z - 1, NZ))
    oshare(md(z + 1, NZ))
    ring_arrive(o_ids)
    o_ids = oring_send(3)
    oshare(md(z - 2, NZ))
    oshare(md(z + 2, NZ))

    wring_arrive(w_ids)
    w_ids = wring_send(2)
    share(1, md(y - 1, NY))
    share(2, md(y + 1, NY))

    ring_arrive(o_ids)
    o_ids = oring_send(4)
    oshare(md(z - 3, NZ))
    oshare(md(z + 3, NZ))

    dn_partner = []
    own_d.wait()
    for i, d in dnx:
        region = DN.at[md(x - d, NX), my_half]
        net.arrive(i, region, dev(dx=-d))
        dn_partner.append((net.send(region, region, partner), d))

    ring_arrive(o_ids)
    oshare(md(z - 4, NZ))
    for i, zb in o_partner:
        net.arrive(i, oblock(zb, 1 - c), partner)

    def project(j, carry):
        cols = pl.ds(pl.multiple_of(j * 256, 256), 256)
        acc = jnp.dot(aperm[...], OW[:, cols], preferred_element_type=f32)
        tok[0, :, cols] = (res[:, cols].astype(f32) + acc).astype(bf16)
        return carry

    lax.fori_loop(0, nt, project, 0)

    def tring_send(s):
        src_f, dst_f = rel_slot(-(s - 1)), rel_slot(-s)
        src_b, dst_b = rel_slot(s - 1), rel_slot(s)
        if s < 4:
            a = net.send(tok.at[src_f], tok.at[dst_f], dev(dz=1))
            b = net.send(tok.at[src_b], tok.at[dst_b], dev(dz=-1))
            return [(a, tok.at[dst_f], -1), (b, tok.at[dst_b], 1)]
        lo, hi = pl.ds(0, T // 2), pl.ds(T // 2, T // 2)
        a = net.send(tok.at[src_f, lo], tok.at[dst_f, lo], dev(dz=1))
        b = net.send(tok.at[src_b, hi], tok.at[dst_b, hi], dev(dz=-1))
        return [(a, tok.at[dst_f, lo], -1), (b, tok.at[dst_b, hi], 1)]

    for i, d in metas:
        net.arrive(i, meta.at[rel_slot(-d)], dev(dz=-d))

    def select(p):
        row = lax.broadcasted_iota(jnp.int32, (PAIR, T), 0).astype(f32)
        for e in range(NX):
            ma = meta[2 * p, e : e + 1, :] == row
            mb = meta[2 * p + 1, e : e + 1, :] + float(CAP) == row
            wa = jnp.where(ma, meta[2 * p, 4 + e : 5 + e, :], 0.0)
            wb = jnp.where(mb, meta[2 * p + 1, 4 + e : 5 + e, :], 0.0)
            sel[p, e, :, 0:T] = jnp.where(ma, 1.0, 0.0).astype(bf16)
            sel[p, e, :, T : 2 * T] = jnp.where(mb, 1.0, 0.0).astype(bf16)
            w = jnp.sum(wa + wb, axis=1, keepdims=True)
            wrow[p, e] = jnp.broadcast_to(w, (PAIR, 128))

    def gather(p, q):
        both = sel[p].reshape(NX * PAIR, 2 * T)

        def tile(j, carry):
            cols = pl.ds(pl.multiple_of(j * 256, 256), 256)
            v = jnp.dot(both, tok[2 * p : 2 * p + 2, :, cols].reshape(2 * T, 256), preferred_element_type=f32)
            X[:, q * PAIR : (q + 1) * PAIR, cols] = v.astype(bf16).reshape(NX, PAIR, 256)
            return carry

        lax.fori_loop(0, nt, tile, 0)

    def experts(pairs):
        def one(e, carry):
            xe = X[e]
            g = jnp.dot(xe, G[e], preferred_element_type=f32)
            u = jnp.dot(xe, U[e], preferred_element_type=f32)
            h = (jax.nn.silu(g) * u).astype(bf16)
            for j in range(F // 512):
                o = jnp.dot(h, DN[e, :, j * 512 : (j + 1) * 512], preferred_element_type=f32)
                for q, p in enumerate(pairs):
                    w = wrow[p, e][:, 0:1]
                    Y[p, e, :, j * 512 : (j + 1) * 512] = (
                        o[q * PAIR : (q + 1) * PAIR, :] * w
                    ).astype(bf16)
            return carry

        lax.fori_loop(0, NX, one, 0)

    t_ids = tring_send(1)
    for p in range(4):
        select(p)

    wring_arrive(w_ids)
    w_ids = wring_send(3)
    share(3, md(y - 2, NY))
    share(4, md(y + 2, NY))

    ring_arrive(t_ids)
    t_ids = tring_send(2)
    gather(1, 0)
    ring_arrive(t_ids)
    t_ids = tring_send(3)
    gather(2, 1)

    wring_arrive(w_ids)
    w_ids = wring_send(4)
    share(5, md(y - 3, NY))
    share(6, md(y + 3, NY))
    ring_arrive(t_ids)
    t_ids = tring_send(4)
    wring_arrive(w_ids)
    share(7, md(y - 4, NY))
    for i, d in dn_partner:
        net.arrive(i, DN.at[md(x - d, NX), pl.ds(pl.multiple_of((1 - c) * half, 8), half)], partner)
    for i, W, yb in to_partner:
        net.arrive(i, wblock(W, yb, 1 - c), partner)

    experts((1, 2))
    gather(3, 0)
    ring_arrive(t_ids)
    gather(0, 1)
    experts((3, 0))

    def mix(slot, b):
        p, h = slot // 2, slot % 2

        def tile(j, carry):
            cols = pl.ds(pl.multiple_of(j * 256, 256), 256)
            part[b, :, cols] = lax.dot_general(
                sel[p, :, :, h * T : (h + 1) * T].reshape(NX * PAIR, T),
                Y[p, :, :, cols].reshape(NX * PAIR, 256),
                (((0,), (0,)), ((), ())),
                preferred_element_type=f32,
            )
            return carry

        lax.fori_loop(0, nt, tile, 0)

    lo, hi = pl.ds(0, T // 2), pl.ds(T // 2, T // 2)
    mix(rel_slot(4), 0)
    SB[0, 0, lo] = part[0, lo].astype(bf16)
    SB[1, 0, hi] = part[0, hi].astype(bf16)
    r_ids = [
        (net.send(SB.at[0, 0, lo], RB.at[0, 0, lo], dev(dz=1)), RB.at[0, 0, lo], -1),
        (net.send(SB.at[1, 0, hi], RB.at[1, 0, hi], dev(dz=-1)), RB.at[1, 0, hi], 1),
    ]
    for s in (2, 3, 4):
        r = 5 - s
        mix(rel_slot(r), 0)
        mix(rel_slot(-r), 1)
        ring_arrive(r_ids)
        r_ids = []
        for b, (side, got) in enumerate(((1, lo), (-1, hi))):
            if s == 2:
                keep = hi if b == 0 else lo
                SB[b, s - 1, keep] = part[b, keep].astype(bf16)
                SB[b, s - 1, got] = (part[b, got] + RB[b, 0, got].astype(f32)).astype(bf16)
            else:
                SB[b, s - 1] = (part[b] + RB[b, s - 2].astype(f32)).astype(bf16)
            r_ids.append((net.send(SB.at[b, s - 1], RB.at[b, s - 1], dev(dz=side)), RB.at[b, s - 1], -side))
    mix(0, 0)
    ring_arrive(r_ids)
    total = tok[0].astype(f32) + (part[0] + RB[0, 3].astype(f32) + RB[1, 3].astype(f32))
    scale = lax.rsqrt(jnp.mean(total * total, axis=1, keepdims=True) + 1e-06)
    out[...] = (total * scale * gain[...]).astype(bf16)
    net.drain()
    assert net.count <= N_COPIES


def row_order():
    z, c, y, x, j = np.meshgrid(
        np.arange(NZ), np.arange(2), np.arange(NY), np.arange(NX), np.arange(3), indexing="ij"
    )
    return (((y * 2 + c) * NX + x) * NZ + z).reshape(-1) * 3 + j.reshape(-1)


def body(attention, residual, out_weight, gate_weight, up_weight, down_weight, routes, router_scores, norm_gain):
    T, F = attention.shape
    rows, H = gate_weight.shape[1:]
    kperm = jnp.asarray(row_order()[None, :], jnp.int32)
    bf16, f32 = jnp.bfloat16, jnp.float32
    vm = pl.BlockSpec(memory_space=pltpu.VMEM)
    hbm = pl.BlockSpec(memory_space=pl.ANY)
    return pl.pallas_call(
        kernel,
        out_shape=jax.ShapeDtypeStruct((T, F), bf16),
        in_specs=[vm, vm, vm, hbm, hbm, hbm, vm, vm, vm, vm],
        out_specs=vm,
        scratch_shapes=[
            pltpu.VMEM((NY, NX, 3, F), bf16),
            pltpu.VMEM((NY * NX * 3, F), f32),
            pltpu.VMEM((F, F), bf16),
            pltpu.VMEM((NX, F, H), bf16),
            pltpu.VMEM((NX, F, H), bf16),
            pltpu.VMEM((NX, H, F), bf16),
            pltpu.VMEM((NZ, T, F), bf16),
            pltpu.VMEM((NZ, 8, T), f32),
            pltpu.VMEM((NZ, 8, T), f32),
            pltpu.VMEM((4, NX, PAIR, 2 * T), bf16),
            pltpu.VMEM((4, NX, PAIR, 128), f32),
            pltpu.VMEM((NX, 2 * PAIR, F), bf16),
            pltpu.VMEM((4, NX, PAIR, F), bf16),
            pltpu.VMEM((2, 4, T, F), bf16),
            pltpu.VMEM((2, 4, T, F), bf16),
            pltpu.VMEM((2, T, F), f32),
            pltpu.VMEM((T, F), bf16),
            pltpu.SemaphoreType.DMA((N_COPIES,)),
            pltpu.SemaphoreType.DMA((N_COPIES,)),
            pltpu.SemaphoreType.DMA((4,)),
        ],
        compiler_params=pltpu.CompilerParams(
            collective_id=0, has_side_effects=True, vmem_limit_bytes=62 * 1024 * 1024
        ),
    )(
        attention, residual, out_weight, gate_weight[0], up_weight[0], down_weight[0],
        routes.T, router_scores.T, norm_gain[None, :], kperm,
    )


def solution(mesh):
    rows = P(("dp", "expert"), None)
    in_specs = (
        rows, rows, rows, P("expert", "dp", None), P("expert", "dp", None), P("expert", None, None),
        rows, rows, P(),
    )
    return jax.shard_map(body, mesh=mesh, in_specs=in_specs, out_specs=rows, check_vma=False)
```

time: 405 us -> 156 us (0.39)
  waiting for transfers between devices: 292 us -> 0 us
  Pallas kernels: 0 us -> 153 us
  local copies, waits for them, and re-layouts: 47.8 us -> 3.06 us
  matrix products: 19.1 us -> 0 us
  starting transfers between devices: 16.5 us -> 0 us
  between operations: 15 us -> 0.01 us
  other arithmetic: 11.7 us -> 0 us
    all_gather x3 -> x0, waiting for transfers between devices: 158 us -> none  [the longest x1 116 us: body(): lax.all_gather(out_weight, ('dp', 'expert'), axis=0, tiled=True)]
    pallas_call x0 -> x1, Pallas kernels: none -> 153 us  [body(): pl.pallas_call(kernel, out_shape=jax.ShapeDtypeStruct((T, F), bf16), in_s...]
    all_to_all x2 -> x0, waiting for transfers between devices: 132 us -> none  [the longest x1 86.7 us: body(): lax.all_to_all(expert_out.reshape(received.shape), 'expert', split_axis=0...]
    dot_general x3 -> x0, matrix products: 19.1 us -> none  [the longest x1 9.65 us: body(): jnp.dot(expert_hidden, down_mat, preferred_element_type=jnp.float32)]
    all_to_all x2 -> x0, starting transfers between devices: 16.4 us -> none  [the longest x1 8.6 us: body(): lax.all_to_all(expert_out.reshape(received.shape), 'expert', split_axis=0...]
    gather x2 -> x0, local copies, waits for them, and re-layouts: 15.4 us -> none  [the longest x1 9.9 us: body(): answered.reshape(-1, feature_count)[target]]
    slice x3 -> x0, local copies, waits for them, and re-layouts: 14.5 us -> none  [the longest x1 14.2 us: body(): picked[:, choice_index].astype(jnp.float32)]
    unnamed x12 -> x1, local copies, waits for them, and re-layouts: 13.1 us -> 1.77 us
  transfers between devices with their start and end apart: 5 -> 0, of which waited for: 4 -> 0; matrix products, arithmetic and copies ran while one was open for 5% -> 0% of each run, Pallas kernels for 0% -> 0%
where the time goes in v1:
time: 156 us
  Pallas kernels  153 us (98%)
  local copies, waits for them, and re-layouts  3.06 us (2%)
    pallas_call x1, Pallas kernels, body(): pl.pallas_call(kernel, out_shape=jax.ShapeDtypeStruct((T, F), bf16), in_s...  153 us

profile of v1, /device:TPU:1, one launch (start us, length us, event | category | flops | bytes accessed | tf_op | source)
XLA Modules:
  0.0 156.0 jit_solution(7600799678402050318)
XLA Ops:
  0.0 1.3 broadcast_in_dim.3.gain
  1.3 152.9 %shard_map.100 = bf16[128,1536]{1,0:T(8,128)(2,1)} custom-call(bf16[128,1536]{1,0:T(8,128)(2,1)} %att.1, bf16[128,1536]{1,0:T(8,128)(2,1)} %res.1, bf16[3,1536]{1,0:T(4,128)(2,1)} %ow.1, bf16[96,512]{1,0:T(8,128)(2,1)} %bitcast.6, bf16[96,512]{1,0:T(8,128)(2,1)} %bitcast.7, bf16[512,1536]{1,0:T(8,128)(2,1)} %bitcast.5, s32[8,128]{1,0:T(8,128)} %bitcast.8, ...), custom_call_target="tpu_custom_call" | custom-call | tf_op jit(solution)/shard_map/pallas_call | solution.py:401
  154.2 1.8 %copy.12 = bf16[128,1536]{1,0:T(8,128)(2,1)} copy(bf16[128,1536]{1,0:T(8,128)(2,1)} %shard_map.100) | data formatting | bytes 786432

commit v2 on v1

v2 whole, which is shorter than its diff:
```python
import jax
import jax.numpy as jnp
import numpy as np
from jax import lax
from jax.experimental import pallas as pl
from jax.experimental.pallas import tpu as pltpu
from jax.sharding import PartitionSpec as P

NX, NY, NZ = 4, 8, 8
CAP = 40
PAIR = 2 * CAP
SLOT = {0: 0, 4: 1, 1: 2, -1: 3, 2: 4, -2: 5, 3: 6, -3: 7}


def rel_slot(r):
    r = r % NZ
    return SLOT[r if r <= 4 else r - NZ]


class Net:
    def __init__(self, send_sems, recv_sems):
        self.ss, self.rs, self.count, self.sent = send_sems, recv_sems, 0, []

    def send(self, src, dst, device):
        i = self.count
        self.count += 1
        copy = pltpu.make_async_remote_copy(
            src_ref=src, dst_ref=dst, send_sem=self.ss.at[i], recv_sem=self.rs.at[i],
            device_id=device, device_id_type=pl.DeviceIdType.MESH,
        )
        copy.start()
        self.sent.append(copy)
        return i

    def arrive(self, i, region, device):
        pltpu.make_async_remote_copy(
            src_ref=region, dst_ref=region, send_sem=self.ss.at[i], recv_sem=self.rs.at[i],
            device_id=device, device_id_type=pl.DeviceIdType.MESH,
        ).wait_recv()

    def drain(self):
        for copy in self.sent:
            copy.wait_send()


N_COPIES = 176
NEAR = 1024


class Ring:
    def __init__(self, net, plus, minus, region, halves, split, relative=False):
        self.net, self.plus, self.minus = net, plus, minus
        self.region, self.halves, self.split, self.relative = region, halves, split, relative
        self.flight = {}

    def parts(self, s):
        lo, hi = self.halves
        if s == 4:
            return [(1, lo), (-1, hi)]
        if self.split:
            return [(1, lo), (-1, hi), (1, hi), (-1, lo)]
        return [(1, None), (-1, None)]

    def push(self, s, way, half):
        ref = self.region(way * (s - 1), half)
        dst = self.region(way * s, half) if self.relative else ref
        i = self.net.send(ref, dst, self.plus if way > 0 else self.minus)
        self.flight.setdefault(s, []).append((i, way, half))

    def start(self):
        for way, half in self.parts(1):
            self.push(1, way, half)

    def advance(self, s):
        for i, way, half in self.flight[s]:
            self.net.arrive(i, self.region(way * s, half), self.minus if way > 0 else self.plus)
            if s < 4:
                for way2, half2 in self.parts(s + 1):
                    if way2 == way and (half is None or half2 == half):
                        self.push(s + 1, way, half2)


def kernel(
    att, res, ow, gate, up, down, routes_t, scores_t, gain, kperm,
    out,
    s1a, s1c, s1f, OWA, OWC, GU, DN, tok, meta, tab, sel, wrow, X, Y, SB, RB, part, aperm,
    send_sems, recv_sems, loc_sems,
):
    f32, bf16 = jnp.float32, jnp.bfloat16
    T, F = att.shape
    rows, H = gate.shape
    KEEP = H + H // 2
    dp, ex = lax.axis_index("dp"), lax.axis_index("expert")
    y, c = lax.div(dp, 2), lax.rem(dp, 2)
    x, z = lax.div(ex, NZ), lax.rem(ex, NZ)

    def md(a, n):
        return lax.rem(a + 2 * n, n)

    def dev(dx=0, dy=0, dz=0, other=False):
        cc = 1 - c if other else c
        return (md(y + dy, NY) * 2 + cc, md(x + dx, NX) * NZ + md(z + dz, NZ))

    partner = dev(other=True)
    net = Net(send_sems, recv_sems)

    def local(k, src, dst):
        copy = pltpu.make_async_copy(src, dst, loc_sems.at[k])
        copy.start()
        return copy

    own_a = local(0, ow.at[:, 0:NEAR], s1a.at[x, y])
    own_c = local(1, ow.at[:, NEAR:F], s1c.at[x, z])
    own_g = local(2, gate, GU.at[x, y, c, :, 0:H])
    own_u = local(3, up, GU.at[x, y, c, :, H : 2 * H])
    own_d = local(4, down, DN.at[x])

    barrier = pltpu.get_barrier_semaphore()
    peers = (
        [dev(dx=d) for d in range(1, NX)] + [dev(dy=d) for d in range(1, NY)]
        + [dev(dz=d) for d in range(1, NZ)] + [partner]
    )
    for p in peers:
        pl.semaphore_signal(barrier, inc=1, device_id=p, device_id_type=pl.DeviceIdType.MESH)

    r8 = lax.broadcasted_iota(jnp.int32, (NZ * 8, T), 0)
    expert_of = (r8 % 4) * NZ + r8 // 8
    scores = scores_t[...]
    combine = scores / jnp.sum(scores, axis=0, keepdims=True)
    member = jnp.zeros((NZ * 8, T), f32)
    weight = jnp.zeros((NZ * 8, T), f32)
    for k in range(routes_t.shape[0]):
        hit = routes_t[k : k + 1, :] == expert_of
        member = member + jnp.where(hit, 1.0, 0.0)
        weight = weight + jnp.where(hit, combine[k : k + 1, :], 0.0)
    before = lax.broadcasted_iota(jnp.int32, (T, T), 0) < lax.broadcasted_iota(jnp.int32, (T, T), 1)
    place = jnp.dot(member.astype(bf16), jnp.where(before, 1.0, 0.0).astype(bf16), preferred_element_type=f32)
    table = jnp.where(r8 % 8 < 4, jnp.where(member > 0.5, place, -1000.0), weight)
    tab[...] = table.reshape(NZ, 8, T)
    meta[0] = tab[z]

    nt = F // 256

    def permute(n):
        def tile(j, carry):
            cols = pl.ds(pl.multiple_of(j * 256, 256), 256)
            onehot = lax.broadcasted_iota(jnp.int32, (F, 256), 0) == kperm[n : n + 1, cols]
            aperm[n, :, cols] = jnp.dot(
                att[...], jnp.where(onehot, 1.0, 0.0).astype(bf16), preferred_element_type=f32
            ).astype(bf16)
            return carry

        lax.fori_loop(0, nt, tile, 0)

    permute(0)
    permute(1)
    pl.semaphore_wait(barrier, len(peers))

    far_first = (4, 3, 5, 2, 6, 1, 7)
    a1 = [(net.send(ow.at[:, 0:NEAR], s1a.at[x, y], dev(dy=d)), d) for d in far_first]
    c1 = [(net.send(ow.at[:, NEAR:F], s1c.at[x, z], dev(dz=d)), d) for d in far_first]

    blk_lo, blk_hi = pl.ds(0, rows // 2), pl.ds(rows // 2, rows // 2)
    full = pl.ds(0, rows)

    def block(e, half=None):
        return GU.at[e, y, c, full if half is None else half, 0:KEEP]

    def piece(e):
        return Ring(
            net, dev(dy=1), dev(dy=-1),
            lambda k, half: GU.at[e, md(y - k, NY), c, full if half is None else half, 0:KEEP],
            (blk_lo, blk_hi), False,
        )

    order = (x, md(x - 1, NX), md(x + 1, NX), md(x + 2, NX))
    pieces = [piece(e) for e in order]
    late = Ring(
        net, dev(dy=1), dev(dy=-1),
        lambda k, half: GU.at[x, md(y - k, NY), c, full if half is None else half, KEEP : 2 * H],
        (blk_lo, blk_hi), False,
    )
    own_g.wait()
    own_u.wait()
    wx = [net.send(block(x), block(x), dev(dx=1)), net.send(block(x), block(x), dev(dx=-1))]
    late.start()
    pieces[0].start()

    own_a.wait()
    for i, d in a1:
        net.arrive(i, s1a.at[x, md(y - d, NY)], dev(dy=-d))
    a2 = [(net.send(s1a.at[x], s1a.at[x], dev(dx=d)), d) for d in (2, 1, 3)]
    own_c.wait()
    for i, d in c1:
        net.arrive(i, s1c.at[x, md(z - d, NZ)], dev(dz=-d))
    c2 = [(net.send(s1c.at[x], s1c.at[x], dev(dx=d)), d) for d in (2, 1, 3)]
    metas = []
    for d in range(1, NZ):
        metas.append((net.send(tab.at[md(z + d, NZ)], meta.at[rel_slot(-d)], dev(dz=d)), d))

    late.advance(1)
    net.arrive(wx[0], block(order[1]), dev(dx=-1))
    net.arrive(wx[1], block(order[2]), dev(dx=1))
    wx2 = [
        net.send(block(order[1], blk_lo), block(order[1], blk_lo), dev(dx=1)),
        net.send(block(order[2], blk_hi), block(order[2], blk_hi), dev(dx=-1)),
    ]
    pieces[1].start()
    late.advance(2)
    late.advance(3)

    own_rows = NY * NX * 3

    def orows(b, cc, half):
        lo, n = (0, own_rows) if half is None else half
        return pl.ds(pl.multiple_of((b * 2 + cc) * own_rows + lo, 8), n)

    ohalves = ((0, own_rows // 2), (own_rows // 2, own_rows // 2))
    ring_a = Ring(
        net, dev(dz=1), dev(dz=-1), lambda k, half: OWA.at[orows(md(z - k, NZ), c, half)], ohalves, True
    )
    ring_c = Ring(
        net, dev(dy=1), dev(dy=-1), lambda k, half: OWC.at[orows(md(y - k, NY), c, half)], ohalves, False
    )

    def collect(s1, dst, b, lo, n):
        for xb in range(NX):
            for q in range(8):
                at = (xb * 8 + q) * 3
                s1f[at : at + 3, lo : lo + n] = s1[xb, q].astype(f32)
        dst[orows(b, c, None), :] = s1f[:, lo : lo + n].astype(bf16)

    o_partner = []

    def oshare(dst, b):
        ref = dst.at[orows(b, c, None)]
        o_partner.append((net.send(ref, ref, partner), dst, b))

    def ashare(s):
        for k in ((s, -s) if 0 < s < 4 else (s,)):
            oshare(OWA, md(z - k, NZ))

    def cshare(s):
        for k in ((s, -s) if 0 < s < 4 else (s,)):
            oshare(OWC, md(y - k, NY))

    for i, d in a2:
        net.arrive(i, s1a.at[md(x - d, NX)], dev(dx=-d))
    collect(s1a, OWA, z, 0, NEAR)
    ring_a.start()
    for i, d in c2:
        net.arrive(i, s1c.at[md(x - d, NX)], dev(dx=-d))
    collect(s1c, OWC, y, NEAR, F - NEAR)
    ring_c.start()
    pieces[2].start()
    ashare(0)
    cshare(0)

    late.advance(4)
    w_partner = [[], [], [], []]

    def lates(e, lo=0, n=NY, cc=None):
        return GU.at[e, pl.ds(lo, n), c if cc is None else cc, :, KEEP : 2 * H]

    def late_share(n):
        e = order[n]
        w_partner[n].append((net.send(lates(e), lates(e), partner), lates(e, cc=1 - c)))

    lx = [net.send(lates(x), lates(x), dev(dx=1)), net.send(lates(x), lates(x), dev(dx=-1))]
    late_share(0)
    half = H // 2

    def drows(e, lo=0, n=half, cc=None):
        return DN.at[e, pl.ds(pl.multiple_of((c if cc is None else cc) * half + lo, 8), n)]

    my_down = down.at[pl.ds(pl.multiple_of(c * half, 8), half)]
    dx = [net.send(my_down, drows(x), dev(dx=1)), net.send(my_down, drows(x), dev(dx=-1))]

    def down_share(n):
        e = order[n]
        w_partner[n].append((net.send(drows(e), drows(e), partner), drows(e, cc=1 - c)))

    net.arrive(wx2[0], block(order[3], blk_lo), dev(dx=-1))
    net.arrive(wx2[1], block(order[3], blk_hi), dev(dx=1))

    def gshare(s):
        for k in ((s, -s) if s else (0,)):
            yb = md(y - k, NY)
            ref = GU.at[:, yb, c, :, 0:KEEP]
            g_partner.append((net.send(ref, ref, partner), GU.at[:, yb, 1 - c, :, 0:KEEP]))

    g_partner = []
    ring_c.advance(1)
    pieces[3].start()
    gshare(0)
    ring_a.advance(1)
    cshare(1)
    ashare(1)
    ring_c.advance(2)
    pieces[0].advance(1)
    ring_a.advance(2)
    cshare(2)
    ashare(2)
    net.arrive(lx[0], lates(order[1]), dev(dx=-1))
    net.arrive(lx[1], lates(order[2]), dev(dx=1))
    lx2 = [
        net.send(lates(order[1], 0, NY // 2), lates(order[1], 0, NY // 2), dev(dx=1)),
        net.send(lates(order[2], NY // 2, NY // 2), lates(order[2], NY // 2, NY // 2), dev(dx=-1)),
    ]
    late_share(1)
    late_share(2)
    ring_c.advance(3)
    ring_a.advance(3)
    for n in (1, 2, 3):
        pieces[n].advance(1)
    cshare(3)
    ashare(3)
    ring_c.advance(4)
    cshare(4)
    ring_a.advance(4)
    ashare(4)
    gshare(1)
    for i, dst, b in o_partner:
        net.arrive(i, dst.at[orows(b, 1 - c, None)], partner)

    def project(W, n, lo, tiles):
        def tile(j, carry):
            cols = pl.ds(pl.multiple_of(j * 256, 256), 256)
            to = pl.ds(pl.multiple_of(lo + j * 256, 256), 256)
            acc = jnp.dot(aperm[n], W[:, cols], preferred_element_type=f32)
            tok[0, :, to] = (res[:, to].astype(f32) + acc).astype(bf16)
            return carry

        lax.fori_loop(0, tiles, tile, 0)

    project(OWA, 0, 0, NEAR // 256)
    project(OWC, 1, NEAR, (F - NEAR) // 256)

    tlo, thi = pl.ds(0, T // 2), pl.ds(T // 2, T // 2)
    ring_t = Ring(
        net, dev(dz=1), dev(dz=-1), lambda k, half: tok.at[rel_slot(-k), half], (tlo, thi), True, True
    )
    ring_t.start()
    for i, d in metas:
        net.arrive(i, meta.at[rel_slot(-d)], dev(dz=-d))

    def select(p):
        row = lax.broadcasted_iota(jnp.int32, (PAIR, T), 0).astype(f32)
        for e in range(NX):
            ma = meta[2 * p, e : e + 1, :] == row
            mb = meta[2 * p + 1, e : e + 1, :] + float(CAP) == row
            wa = jnp.where(ma, meta[2 * p, 4 + e : 5 + e, :], 0.0)
            wb = jnp.where(mb, meta[2 * p + 1, 4 + e : 5 + e, :], 0.0)
            sel[p, e, :, 0:T] = jnp.where(ma, 1.0, 0.0).astype(bf16)
            sel[p, e, :, T : 2 * T] = jnp.where(mb, 1.0, 0.0).astype(bf16)
            w = jnp.sum(wa + wb, axis=1, keepdims=True)
            wrow[p, e] = jnp.broadcast_to(w, (PAIR, 128))

    def gather(p, q):
        both = sel[p].reshape(NX * PAIR, 2 * T)

        def tile(j, carry):
            cols = pl.ds(pl.multiple_of(j * 256, 256), 256)
            v = jnp.dot(both, tok[2 * p : 2 * p + 2, :, cols].reshape(2 * T, 256), preferred_element_type=f32)
            X[:, q * PAIR : (q + 1) * PAIR, cols] = v.astype(bf16).reshape(NX, PAIR, 256)
            return carry

        lax.fori_loop(0, nt, tile, 0)

    def expert(pairs, e):
        gu = jnp.dot(X[e], GU[e].reshape(F, 2 * H), preferred_element_type=f32)
        h = (jax.nn.silu(gu[:, 0:H]) * gu[:, H : 2 * H]).astype(bf16)
        for j in range(F // 512):
            o = jnp.dot(h, DN[e, :, j * 512 : (j + 1) * 512], preferred_element_type=f32)
            for q, p in enumerate(pairs):
                w = wrow[p, e][:, 0:1]
                Y[p, e, :, j * 512 : (j + 1) * 512] = (o[q * PAIR : (q + 1) * PAIR, :] * w).astype(bf16)

    for p in range(4):
        select(p)
    for ring in pieces:
        ring.advance(2)
    gshare(2)
    own_d.wait()
    net.arrive(dx[0], drows(order[1]), dev(dx=-1))
    net.arrive(dx[1], drows(order[2]), dev(dx=1))
    dx2 = [
        net.send(drows(order[1], 0, half // 2), drows(order[1], 0, half // 2), dev(dx=1)),
        net.send(drows(order[2], half // 2, half // 2), drows(order[2], half // 2, half // 2), dev(dx=-1)),
    ]
    down_share(1)
    down_share(2)
    ring_t.advance(1)
    net.arrive(lx2[0], lates(order[3], 0, NY // 2), dev(dx=-1))
    net.arrive(lx2[1], lates(order[3], NY // 2, NY // 2), dev(dx=1))
    late_share(3)
    for ring in pieces:
        ring.advance(3)
    gshare(3)
    ring_t.advance(2)
    net.arrive(dx2[0], drows(order[3], 0, half // 2), dev(dx=-1))
    net.arrive(dx2[1], drows(order[3], half // 2, half // 2), dev(dx=1))
    down_share(3)
    for n, ring in enumerate(pieces):
        ring.advance(4)
        far = md(y - 4, NY)
        ref = GU.at[order[n], far, c, :, 0:KEEP]
        w_partner[n].append((net.send(ref, ref, partner), GU.at[order[n], far, 1 - c, :, 0:KEEP]))
    ring_t.advance(3)
    gather(3, 0)
    ring_t.advance(4)
    gather(0, 1)
    for i, ref in g_partner:
        net.arrive(i, ref, partner)
    for n in range(NX):
        for i, ref in w_partner[n]:
            net.arrive(i, ref, partner)
        expert((3, 0), order[n])

    def mix(slot, b):
        p, h = slot // 2, slot % 2

        def tile(j, carry):
            cols = pl.ds(pl.multiple_of(j * 256, 256), 256)
            part[b, :, cols] = lax.dot_general(
                sel[p, :, :, h * T : (h + 1) * T].reshape(NX * PAIR, T),
                Y[p, :, :, cols].reshape(NX * PAIR, 256),
                (((0,), (0,)), ((), ())),
                preferred_element_type=f32,
            )
            return carry

        lax.fori_loop(0, nt, tile, 0)

    def rsend(s, b, half):
        i = net.send(SB.at[b, s - 1, half], RB.at[b, s - 1, half], dev(dz=1 if b == 0 else -1))
        return (i, b, half)

    def rarrive(s, flight):
        i, b, half = flight
        net.arrive(i, RB.at[b, s - 1, half], dev(dz=-1 if b == 0 else 1))

    mix(rel_slot(4), 0)
    r_ids = []
    for b, half in ((0, tlo), (1, thi)):
        SB[b, 0, half] = part[0, half].astype(bf16)
        r_ids.append(rsend(1, b, half))
    mix(rel_slot(3), 0)
    mix(rel_slot(-3), 1)
    new = []
    for b, half in ((0, thi), (1, tlo)):
        SB[b, 1, half] = part[b, half].astype(bf16)
        new.append(rsend(2, b, half))
    gather(1, 0)
    gather(2, 1)

    def one(e, carry):
        expert((1, 2), e)
        return carry

    lax.fori_loop(0, NX, one, 0)
    for s in (2, 3, 4):
        if s > 2:
            r = 5 - s
            mix(rel_slot(r), 0)
            mix(rel_slot(-r), 1)
            new = []
        for flight in r_ids:
            _, b, half = flight
            rarrive(s - 1, flight)
            SB[b, s - 1, half] = (part[b, half] + RB[b, s - 2, half].astype(f32)).astype(bf16)
            new.append(rsend(s, b, half))
        r_ids = new
    mix(0, 0)
    for flight in r_ids:
        rarrive(4, flight)
    total = tok[0].astype(f32) + (part[0] + RB[0, 3].astype(f32) + RB[1, 3].astype(f32))
    scale = lax.rsqrt(jnp.mean(total * total, axis=1, keepdims=True) + 1e-06)
    out[...] = (total * scale * gain[...]).astype(bf16)
    net.drain()
    assert net.count <= N_COPIES


def row_order():
    def order(*axes):
        g = dict(zip(axes, np.meshgrid(*[np.arange(SIZE[a]) for a in axes], indexing="ij")))
        return ((((g["y"] * 2 + g["c"]) * NX + g["x"]) * NZ + g["z"]) * 3 + g["j"]).reshape(-1)

    return np.stack([order("z", "c", "x", "y", "j"), order("y", "c", "x", "z", "j")])


SIZE = {"x": NX, "y": NY, "z": NZ, "c": 2, "j": 3}


def body(attention, residual, out_weight, gate_weight, up_weight, down_weight, routes, router_scores, norm_gain):
    T, F = attention.shape
    rows, H = gate_weight.shape[1:]
    kperm = jnp.asarray(row_order(), jnp.int32)
    bf16, f32 = jnp.bfloat16, jnp.float32
    vm = pl.BlockSpec(memory_space=pltpu.VMEM)
    hbm = pl.BlockSpec(memory_space=pl.ANY)
    return pl.pallas_call(
        kernel,
        out_shape=jax.ShapeDtypeStruct((T, F), bf16),
        in_specs=[vm, vm, vm, hbm, hbm, hbm, vm, vm, vm, vm],
        out_specs=vm,
        scratch_shapes=[
            pltpu.VMEM((NX, NY, 3, NEAR), bf16),
            pltpu.VMEM((NX, NZ, 3, F - NEAR), bf16),
            pltpu.VMEM((NY * NX * 3, F), f32),
            pltpu.VMEM((F, NEAR), bf16),
            pltpu.VMEM((F, F - NEAR), bf16),
            pltpu.VMEM((NX, NY, 2, rows, 2 * H), bf16),
            pltpu.VMEM((NX, H, F), bf16),
            pltpu.VMEM((NZ, T, F), bf16),
            pltpu.VMEM((NZ, 8, T), f32),
            pltpu.VMEM((NZ, 8, T), f32),
            pltpu.VMEM((4, NX, PAIR, 2 * T), bf16),
            pltpu.VMEM((4, NX, PAIR, 128), f32),
            pltpu.VMEM((NX, 2 * PAIR, F), bf16),
            pltpu.VMEM((4, NX, PAIR, F), bf16),
            pltpu.VMEM((2, 4, T, F), bf16),
            pltpu.VMEM((2, 4, T, F), bf16),
            pltpu.VMEM((2, T, F), f32),
            pltpu.VMEM((2, T, F), bf16),
            pltpu.SemaphoreType.DMA((N_COPIES,)),
            pltpu.SemaphoreType.DMA((N_COPIES,)),
            pltpu.SemaphoreType.DMA((5,)),
        ],
        compiler_params=pltpu.CompilerParams(
            collective_id=0, has_side_effects=True, vmem_limit_bytes=62 * 1024 * 1024
        ),
    )(
        attention, residual, out_weight, gate_weight[0], up_weight[0], down_weight[0],
        routes.T, router_scores.T, norm_gain[None, :], kperm,
    )


def solution(mesh):
    rows = P(("dp", "expert"), None)
    in_specs = (
        rows, rows, rows, P("expert", "dp", None), P("expert", "dp", None), P("expert", None, None),
        rows, rows, P(),
    )
    return jax.shard_map(body, mesh=mesh, in_specs=in_specs, out_specs=rows, check_vma=False)
```

time: 156 us -> 129 us (0.83)
  Pallas kernels: 153 us -> 125 us
    pallas_call x1, Pallas kernels: 153 us -> 125 us  [body(): pl.pallas_call(kernel, out_shape=jax.ShapeDtypeStruct((T, F), bf16), in_s...]
where the time goes in v2:
time: 129 us; the launch traced here: 128 us
  Pallas kernels  125 us (97%)
  local copies, waits for them, and re-layouts  3.06 us (2%)
    pallas_call x1, Pallas kernels, body(): pl.pallas_call(kernel, out_shape=jax.ShapeDtypeStruct((T, F), bf16), in_s...  125 us

profile of v2, /device:TPU:1, one launch (start us, length us, event | category | flops | bytes accessed | tf_op | source)
XLA Modules:
  0.0 127.9 jit_solution(2905162921529522078)
XLA Ops:
  0.0 1.3 %broadcast_in_dim.3.gain = f32[1,1536]{1,0:T(1,128)} reshape(f32[1536]{0:T(1024)} %param.18) | data formatting | bytes 12288 | tf_op jit(solution)/shard_map/broadcast_in_dim | solution.py:535
  1.3 124.9 %shard_map.100 = bf16[128,1536]{1,0:T(8,128)(2,1)} custom-call(bf16[128,1536]{1,0:T(8,128)(2,1)} %att.1, bf16[128,1536]{1,0:T(8,128)(2,1)} %res.1, bf16[3,1536]{1,0:T(4,128)(2,1)} %ow.1, bf16[96,512]{1,0:T(8,128)(2,1)} %bitcast.6, bf16[96,512]{1,0:T(8,128)(2,1)} %bitcast.7, bf16[512,1536]{1,0:T(8,128)(2,1)} %bitcast.5, s32[8,128]{1,0:T(8,128)} %bitcast.8, ...), custom_call_target="tpu_custom_call" | custom-call | tf_op jit(solution)/shard_map/pallas_call | solution.py:502
  126.2 1.8 %copy.12 = bf16[128,1536]{1,0:T(8,128)(2,1)} copy(bf16[128,1536]{1,0:T(8,128)(2,1)} %shard_map.100) | data formatting | bytes 786432
